TPU v7x, 128 devices: a whole 4x4x4 slice. The times are simulated.
128 devices in a mesh: blk: 16 (over x_hi, z, core), user: 8 (over y, x_lo).
Axes of the slice: x: 4 (x_hi: 2, x_lo: 2; x = x_hi * 2 + x_lo), y: 4, z: 4, core: 2. Of those that a mesh axis runs over, the one named last changes fastest.
Arguments:
- user_factors: float32 [524288, 256], P(('blk', 'user')), may hold values from -2 to 2
- item_factors: float32 [16384, 256], P(('blk', 'user')), may hold values from -2 to 2
- block_index: int32 [3, 1024, 2, 4], P(None, ('blk', 'user')), may hold values from 0 to 15, as said below
- block_count: int32 [3, 1024, 2], P(None, ('blk', 'user')), may hold values from 1 to 4
- ratings: int32 [3, 1024, 2, 4, 128, 128], P(None, ('blk', 'user')), may hold values from 0 to 10
Outputs:
- users_out: float32 [524288, 256], P(('blk', 'user'))
- items_out: float32 [16384, 256], P(('blk', 'user'))
Inputs may be any that keep to these rules, and one draw needn't show every extreme that they name: `block_index`: the 4 block numbers of one tile are distinct.
All inputs are finite; a program needn't handle non-finite values.
Results may differ from a plain program's by a relative error of at most 0.0003.
Values sent between devices are 32-bit elements; how exact they have to be, the bound alone decides.
A program may use at most 128 MiB of HBM per device.

v0:
```python
import jax
import jax.numpy as jnp
from jax import lax
from jax.sharding import PartitionSpec as P

STEPS = 3


user_rate = 0.01
item_rate = 0.0015
decay_rate = 0.05


def passed_along(block, axis, distance):
    devices = range(lax.axis_size(axis))
    route = [((i - distance) % len(devices), i) for i in devices]
    return lax.ppermute(block, axis, route)


def local_grads(user_rows, item_group, tile_index, tile_count, tile_ratings):
    tile_rows = tile_index.shape[0]
    tile_cols = tile_index.shape[1]
    slots = tile_index.shape[2]
    rank = user_rows.shape[1]
    block = tile_ratings.shape[-1]
    parts = user_rows.shape[0] // (tile_rows * block)
    sub_row = tile_index // parts
    sub_col = tile_index % parts
    user_tiles = user_rows.reshape(tile_rows, parts, block, rank)
    item_tiles = item_group.reshape(tile_cols, parts, block, rank)
    row_ids = jnp.arange(tile_rows)[:, None, None]
    col_ids = jnp.arange(tile_cols)[None, :, None]
    user_blocks = user_tiles[row_ids, sub_row]
    item_blocks = item_tiles[col_ids, sub_col]
    predicted = jnp.einsum(
        "abkir,abkjr->abkij", user_blocks, item_blocks, precision=lax.Precision.HIGHEST
    )
    slot_ids = jnp.arange(slots)[None, None, :, None, None]
    observed = (tile_ratings > 0) & (slot_ids < tile_count[:, :, None, None, None])
    residuals = jnp.where(observed, 0.5 * tile_ratings.astype(jnp.float32) - predicted, 0.0)
    user_terms = jnp.einsum(
        "abkij,abkjr->abkir", residuals, item_blocks, precision=lax.Precision.HIGHEST
    )
    item_terms = jnp.einsum(
        "abkij,abkir->abkjr", residuals, user_blocks, precision=lax.Precision.HIGHEST
    )
    part_ids = jnp.arange(parts)
    row_hot = (sub_row[..., None] == part_ids).astype(jnp.float32)
    col_hot = (sub_col[..., None] == part_ids).astype(jnp.float32)
    grad_users = jnp.einsum(
        "abko,abkir->aoir", row_hot, user_terms, precision=lax.Precision.HIGHEST
    )
    grad_items = jnp.einsum(
        "abko,abkjr->bojr", col_hot, item_terms, precision=lax.Precision.HIGHEST
    )
    return (grad_users.reshape(user_rows.shape), grad_items.reshape(item_group.shape))


def local(user_factors, item_factors, block_index, block_count, ratings):
    user_rows = user_factors
    own_items = item_factors
    for step in range(STEPS):
        item_group = lax.all_gather(own_items, "user", axis=0, tiled=True)
        grad_u, grad_v = local_grads(
            user_rows, item_group, block_index[step], block_count[step], ratings[step]
        )
        grad_mine = lax.psum_scatter(grad_v, "user", scatter_dimension=0, tiled=True)
        user_rows = user_rows + user_rate * (grad_u - decay_rate * user_rows)
        change = item_rate * (grad_mine - decay_rate * own_items)
        own_items = passed_along(own_items + change, "blk", 1)
    return (user_rows, own_items)


def solution(mesh):
    in_specs = (
        P(("blk", "user"), None),
        P(("blk", "user"), None),
        P(None, ("blk", "user"), None, None),
        P(None, ("blk", "user"), None),
        P(None, ("blk", "user"), None, None, None, None),
    )
    out_specs = (P(("blk", "user"), None), P(("blk", "user"), None))
    return jax.shard_map(local, mesh=mesh, in_specs=in_specs, out_specs=out_specs, check_vma=False)
```

profile of v0, /device:TPU:1, one launch (start us, length us, event | category | flops | bytes accessed | tf_op | source)
XLA Modules:
  0.0 416.9 jit_solution(12131333598216935546)
XLA Ops:
  9.9 6.5 %gather_fusion = f32[64,128,256]{2,1,0:T(8,128)} fusion(f32[8,4,128,256]{3,2,1,0:T(8,128)} %bitcast.290, s32[64]{0:T(128)S(1)} %reshape.504), kind=kCustom, calls=%fused_computation | custom fusion | bytes 16777728 | tf_op jit(solution)/shard_map/gather | solution.py:33
  16.5 31.5 %all-gather.4.cloned.1.call-done = f32[1024,256]{1,0:T(8,128)} async-done(((f32[128,256]{1,0:T(8,128)}), f32[1024,256]{1,0:T(8,128)}) %all-gather.4.cloned.1.call-update) | async-done | bytes 1048592 | tf_op jit(solution)/shard_map/all_gather | solution.py:63
  53.6 16.3 %fusion.20 = f32[8,2,4,128,128]{4,3,2,1,0:T(8,128)S(1)} fusion(s32[3,8,2,4,128,128]{5,4,3,2,1,0:T(8,128)} %param.9, f32[8,2,4,128,256]{4,3,2,1,0:T(8,128)} %bitcast.279, f32[8,2,4,128,256]{4,3,2,1,0:T(8,128)} %bitcast.275, pred[8,2,4]{2,1,0:T(4,128)(4,1)S(1)} %iota_compare_fusion.8), kind=kOutput, calls=%fused_computation.32 | convolution fusion | flops 3227516928 | bytes 25165888 | tf_op jit(solution)/shard_map/abkir,abkjr->abkij/dot_general | solution.py:35
  69.9 12.3 %fusion.88 = f32[8,2,4,128,256]{4,3,2,1,0:T(8,128)S(1)} fusion(f32[8,2,4,128,128]{4,3,2,1,0:T(8,128)S(1)} %fusion.20, f32[8,2,4,128,256]{4,3,2,1,0:T(8,128)} %bitcast.280), kind=kOutput, calls=%fused_computation.156 | convolution fusion | flops 3221225472 | bytes 20971520 | tf_op jit(solution)/shard_map/abkij,abkir->abkjr/dot_general | solution.py:44
  82.3 8.1 %fusion.30 = f32[2,4,128,256]{3,1,2,0:T(4,128)S(1)} fusion(f32[8,2,4,128,256]{4,3,2,1,0:T(8,128)S(1)} %fusion.88, s32[8,2,4]{0,2,1:T(4,128)S(1)} %get-tuple-element.4), kind=kOutput, calls=%fused_computation.39 | convolution fusion | flops 100663552 | bytes 9437440 | tf_op jit(solution)/shard_map/abko,abkjr->bojr/dot_general | solution.py:53
  92.3 40.7 %reduce-scatter.4.cloned.1.call-done = f32[128,256]{1,0:T(8,128)} async-done(((f32[1024,256]{1,0:T(8,128)}), f32[128,256]{1,0:T(8,128)}) %reduce-scatter.4.cloned.1.call-update) | async-done | bytes 131088 | tf_op jit(solution)/shard_map/reduce_scatter | solution.py:67
  133.9 6.9 %collective-permute-start = (f32[128,256]{1,0:T(8,128)S(1)}, f32[128,256]{1,0:T(8,128)S(1)}, u32[]{:S(2)}, u32[]{:S(2)}) collective-permute-start(f32[128,256]{1,0:T(8,128)S(1)} %multiply_add_fusion.2), channel_id=1, source_target_pairs={{120,0},{0,8},{8,16},{16,24},{24,32},{32,40},{40,48},{48,56},{56,6... | collective-permute-start | bytes 393224 | tf_op jit(solution)/shard_map/ppermute | solution.py:17
  143.4 11.8 %fusion.87 = f32[8,2,4,128,256]{4,3,2,1,0:T(8,128)S(1)} fusion(f32[8,2,4,128,128]{4,3,2,1,0:T(8,128)} %copy-done.3, f32[8,2,4,128,256]{4,3,2,1,0:T(8,128)} %bitcast.276), kind=kOutput, calls=%fused_computation.155 | convolution fusion | flops 3221225472 | bytes 20971520 | tf_op jit(solution)/shard_map/abkij,abkjr->abkir/dot_general | solution.py:41
  155.2 10.7 %fusion.21 = f32[8,4,128,256]{3,1,2,0:T(4,128)S(1)} fusion(f32[8,2,4,128,256]{4,3,2,1,0:T(8,128)S(1)} %fusion.87, s32[8,2,4]{2,1,0:T(2,128)S(1)} %copy.19), kind=kOutput, calls=%fused_computation.36 | convolution fusion | flops 100663552 | bytes 12583168 | tf_op jit(solution)/shard_map/abko,abkir->aoir/dot_general | solution.py:50
  171.5 6.5 %gather_fusion.2 = f32[64,128,256]{2,1,0:T(8,128)} fusion(f32[8,4,128,256]{3,2,1,0:T(8,128)} %bitcast.285, s32[64]{0:T(128)S(1)} %reshape.516), kind=kCustom, calls=%fused_computation.2 | custom fusion | bytes 16777728 | tf_op jit(solution)/shard_map/gather | solution.py:33
  184.7 16.3 %fusion.17 = f32[8,2,4,128,128]{4,3,2,1,0:T(8,128)S(1)} fusion(s32[3,8,2,4,128,128]{5,4,3,2,1,0:T(8,128)} %param.9, f32[8,2,4,128,256]{4,3,2,1,0:T(8,128)} %bitcast.281, f32[8,2,4,128,256]{4,3,2,1,0:T(8,128)} %bitcast.273, pred[8,2,4]{2,1,0:T(4,128)(4,1)S(1)} %iota_compare_fusion.7), kind=kOutput, calls=%fused_computation.27 | convolution fusion | flops 3227516928 | bytes 25165888 | tf_op jit(solution)/shard_map/abkir,abkjr->abkij/dot_general | solution.py:35
  201.0 12.3 %fusion.90 = f32[8,2,4,128,256]{4,3,2,1,0:T(8,128)S(1)} fusion(f32[8,2,4,128,128]{4,3,2,1,0:T(8,128)S(1)} %fusion.17, f32[8,2,4,128,256]{4,3,2,1,0:T(8,128)} %bitcast.282), kind=kOutput, calls=%fused_computation.158 | convolution fusion | flops 3221225472 | bytes 20971520 | tf_op jit(solution)/shard_map/abkij,abkir->abkjr/dot_general | solution.py:44
  213.3 8.1 %fusion.33 = f32[2,4,128,256]{3,1,2,0:T(4,128)S(1)} fusion(f32[8,2,4,128,256]{4,3,2,1,0:T(8,128)S(1)} %fusion.90, s32[8,2,4]{0,2,1:T(4,128)S(1)} %get-tuple-element.3), kind=kOutput, calls=%fused_computation.40 | convolution fusion | flops 100663552 | bytes 9437440 | tf_op jit(solution)/shard_map/abko,abkjr->bojr/dot_general | solution.py:53
  223.3 40.6 %reduce-scatter.6.cloned.1.call-done = f32[128,256]{1,0:T(8,128)} async-done(((f32[1024,256]{1,0:T(8,128)}), f32[128,256]{1,0:T(8,128)}) %reduce-scatter.6.cloned.1.call-update) | async-done | bytes 131088 | tf_op jit(solution)/shard_map/reduce_scatter | solution.py:67
  264.9 6.9 %collective-permute-start.1 = (f32[128,256]{1,0:T(8,128)S(1)}, f32[128,256]{1,0:T(8,128)S(1)}, u32[]{:S(2)}, u32[]{:S(2)}) collective-permute-start(f32[128,256]{1,0:T(8,128)S(1)} %multiply_add_fusion.1), channel_id=1, source_target_pairs={{120,0},{0,8},{8,16},{16,24},{24,32},{32,40},{40,48},{48,56},{56,6... | collective-permute-start | bytes 393224 | tf_op jit(solution)/shard_map/ppermute | solution.py:17
  274.4 11.8 %fusion.89 = f32[8,2,4,128,256]{4,3,2,1,0:T(8,128)S(1)} fusion(f32[8,2,4,128,128]{4,3,2,1,0:T(8,128)} %copy-done.2, f32[8,2,4,128,256]{4,3,2,1,0:T(8,128)} %bitcast.274), kind=kOutput, calls=%fused_computation.157 | convolution fusion | flops 3221225472 | bytes 20971520 | tf_op jit(solution)/shard_map/abkij,abkjr->abkir/dot_general | solution.py:41
  286.2 10.7 %fusion.24 = f32[8,4,128,256]{3,1,2,0:T(4,128)S(1)} fusion(f32[8,2,4,128,256]{4,3,2,1,0:T(8,128)S(1)} %fusion.89, s32[8,2,4]{2,1,0:T(2,128)S(1)} %copy.24), kind=kOutput, calls=%fused_computation.37 | convolution fusion | flops 100663552 | bytes 12583168 | tf_op jit(solution)/shard_map/abko,abkir->aoir/dot_general | solution.py:50
  315.7 16.3 %fusion.14 = f32[8,2,4,128,128]{4,3,2,1,0:T(8,128)S(1)} fusion(s32[3,8,2,4,128,128]{5,4,3,2,1,0:T(8,128)} %param.9, f32[8,2,4,128,256]{4,3,2,1,0:T(8,128)} %bitcast.283, f32[8,2,4,128,256]{4,3,2,1,0:T(8,128)} %bitcast.277, pred[8,2,4]{2,1,0:T(4,128)(4,1)S(1)} %iota_compare_fusion.6), kind=kOutput, calls=%fused_computation.22 | convolution fusion | flops 3227516928 | bytes 25165888 | tf_op jit(solution)/shard_map/abkir,abkjr->abkij/dot_general | solution.py:35
  332.0 12.3 %fusion.92 = f32[8,2,4,128,256]{4,3,2,1,0:T(8,128)S(1)} fusion(f32[8,2,4,128,128]{4,3,2,1,0:T(8,128)S(1)} %fusion.14, f32[8,2,4,128,256]{4,3,2,1,0:T(8,128)} %bitcast.284), kind=kOutput, calls=%fused_computation.160 | convolution fusion | flops 3221225472 | bytes 20971520 | tf_op jit(solution)/shard_map/abkij,abkir->abkjr/dot_general | solution.py:44
  344.3 8.1 %fusion.36 = f32[2,4,128,256]{3,1,2,0:T(4,128)S(1)} fusion(f32[8,2,4,128,256]{4,3,2,1,0:T(8,128)S(1)} %fusion.92, s32[8,2,4]{0,2,1:T(4,128)S(1)} %get-tuple-element.2), kind=kOutput, calls=%fused_computation.41 | convolution fusion | flops 100663552 | bytes 9437440 | tf_op jit(solution)/shard_map/abko,abkjr->bojr/dot_general | solution.py:53
  353.8 11.6 %fusion.91 = f32[8,2,4,128,256]{4,3,2,1,0:T(8,128)S(1)} fusion(f32[8,2,4,128,128]{4,3,2,1,0:T(8,128)} %copy-done.4, f32[8,2,4,128,256]{4,3,2,1,0:T(8,128)} %bitcast.278), kind=kOutput, calls=%fused_computation.159 | convolution fusion | flops 3221225472 | bytes 20971520 | tf_op jit(solution)/shard_map/abkij,abkjr->abkir/dot_general | solution.py:41
  365.4 10.7 %fusion.27 = f32[8,4,128,256]{3,1,2,0:T(4,128)S(1)} fusion(f32[8,2,4,128,256]{4,3,2,1,0:T(8,128)S(1)} %fusion.91, s32[8,2,4]{2,1,0:T(2,128)S(1)} %copy.30), kind=kOutput, calls=%fused_computation.38 | convolution fusion | flops 100663552 | bytes 12583168 | tf_op jit(solution)/shard_map/abko,abkir->aoir/dot_general | solution.py:50
  378.8 16.1 %reduce-scatter.8.cloned.1.call-done = f32[128,256]{1,0:T(8,128)} async-done(((f32[1024,256]{1,0:T(8,128)}), f32[128,256]{1,0:T(8,128)}) %reduce-scatter.8.cloned.1.call-update) | async-done | bytes 131088 | tf_op jit(solution)/shard_map/reduce_scatter | solution.py:67
  395.9 6.9 %collective-permute-start.2 = (f32[128,256]{1,0:T(8,128)S(1)}, f32[128,256]{1,0:T(8,128)S(1)}, u32[]{:S(2)}, u32[]{:S(2)}) collective-permute-start(f32[128,256]{1,0:T(8,128)S(1)} %multiply_add_fusion), channel_id=1, source_target_pairs={{120,0},{0,8},{8,16},{16,24},{24,32},{32,40},{40,48},{48,56},{56,6... | collective-permute-start | bytes 393224 | tf_op jit(solution)/shard_map/ppermute | solution.py:17
  (80 shorter events, 62.2 us)
Async XLA Ops:
  7.2 40.9 %all-gather.4.cloned.1.call-start = ((), (), s32[]{:S(2)}) async-start(), calls=%async_computation.3 | async-start | bytes 1179648 | tf_op jit(solution)/shard_map/all_gather | solution.py:63
  7.9 125.0 %reduce-scatter.4.cloned.1.call-start = ((), (), s32[]{:S(2)}) async-start(), calls=%async_computation.4 | async-start | bytes 1179648 | tf_op jit(solution)/shard_map/reduce_scatter | solution.py:67
  9.9 6.6 %copy-start.10 = (s32[3,8,2,4]{1,3,2,0:T(4,128)S(1)}, s32[3,8,2,4]{1,3,2,0:T(4,128)}, u32[]{:S(2)}) copy-start(s32[3,8,2,4]{1,3,2,0:T(4,128)} %param.7) | copy-start | bytes 2308
  69.9 12.4 %copy-start.3 = (f32[8,2,4,128,128]{4,3,2,1,0:T(8,128)}, f32[8,2,4,128,128]{4,3,2,1,0:T(8,128)S(1)}, u32[]{:S(2)}) copy-start(f32[8,2,4,128,128]{4,3,2,1,0:T(8,128)S(1)} %fusion.20) | copy-start | bytes 12582916
  82.2 50.7 %copy-start.5 = (f32[128,256]{1,0:T(8,128)S(1)}, f32[128,256]{1,0:T(8,128)}, u32[]{:S(2)}) copy-start(f32[128,256]{1,0:T(8,128)} %param.6) | copy-start | bytes 393220
  91.7 87.4 %all-gather.6.cloned.1.call-start = ((), (), s32[]{:S(2)}) async-start(), calls=%async_computation.5 | async-start | bytes 1179648 | tf_op jit(solution)/shard_map/all_gather | solution.py:63
  133.9 8.8 %collective-permute-start = (f32[128,256]{1,0:T(8,128)S(1)}, f32[128,256]{1,0:T(8,128)S(1)}, u32[]{:S(2)}, u32[]{:S(2)}) collective-permute-start(f32[128,256]{1,0:T(8,128)S(1)} %multiply_add_fusion.2), channel_id=1, source_target_pairs={{120,0},{0,8},{8,16},{16,24},{24,32},{32,40},{40,48},{48,56},{56,6... | collective-permute-start | bytes 393224 | tf_op jit(solution)/shard_map/ppermute | solution.py:17
  142.7 0.7 copy-start.6
  143.4 120.6 %reduce-scatter.6.cloned.1.call-start = ((), (), s32[]{:S(2)}) async-start(), calls=%async_computation.6 | async-start | bytes 1179648 | tf_op jit(solution)/shard_map/reduce_scatter | solution.py:67
  165.9 2.2 copy-start.1
  201.0 12.3 %copy-start.2 = (f32[8,2,4,128,128]{4,3,2,1,0:T(8,128)}, f32[8,2,4,128,128]{4,3,2,1,0:T(8,128)S(1)}, u32[]{:S(2)}) copy-start(f32[8,2,4,128,128]{4,3,2,1,0:T(8,128)S(1)} %fusion.17) | copy-start | bytes 12582916
  213.3 50.6 %copy-start.7 = (f32[128,256]{1,0:T(8,128)S(1)}, f32[128,256]{1,0:T(8,128)}, u32[]{:S(2)}) copy-start(f32[128,256]{1,0:T(8,128)} %copy-done.6) | copy-start | bytes 393220
  222.7 87.4 %all-gather.8.cloned.1.call-start = ((), (), s32[]{:S(2)}) async-start(), calls=%async_computation.7 | async-start | bytes 1179648 | tf_op jit(solution)/shard_map/all_gather | solution.py:63
  264.9 8.8 %collective-permute-start.1 = (f32[128,256]{1,0:T(8,128)S(1)}, f32[128,256]{1,0:T(8,128)S(1)}, u32[]{:S(2)}, u32[]{:S(2)}) collective-permute-start(f32[128,256]{1,0:T(8,128)S(1)} %multiply_add_fusion.1), channel_id=1, source_target_pairs={{120,0},{0,8},{8,16},{16,24},{24,32},{32,40},{40,48},{48,56},{56,6... | collective-permute-start | bytes 393224 | tf_op jit(solution)/shard_map/ppermute | solution.py:17
  273.7 0.7 copy-start.8
  274.4 120.6 %reduce-scatter.8.cloned.1.call-start = ((), (), s32[]{:S(2)}) async-start(), calls=%async_computation.8 | async-start | bytes 1179648 | tf_op jit(solution)/shard_map/reduce_scatter | solution.py:67
  296.9 2.2 copy-start
  332.0 12.3 %copy-start.4 = (f32[8,2,4,128,128]{4,3,2,1,0:T(8,128)}, f32[8,2,4,128,128]{4,3,2,1,0:T(8,128)S(1)}, u32[]{:S(2)}) copy-start(f32[8,2,4,128,128]{4,3,2,1,0:T(8,128)S(1)} %fusion.14) | copy-start | bytes 12582916
  376.2 18.8 %copy-start.9 = (f32[128,256]{1,0:T(8,128)S(1)}, f32[128,256]{1,0:T(8,128)}, u32[]{:S(2)}) copy-start(f32[128,256]{1,0:T(8,128)} %copy-done.8) | copy-start | bytes 393220
  395.9 13.0 %collective-permute-start.2 = (f32[128,256]{1,0:T(8,128)S(1)}, f32[128,256]{1,0:T(8,128)S(1)}, u32[]{:S(2)}, u32[]{:S(2)}) collective-permute-start(f32[128,256]{1,0:T(8,128)S(1)} %multiply_add_fusion), channel_id=1, source_target_pairs={{120,0},{0,8},{8,16},{16,24},{24,32},{32,40},{40,48},{48,56},{56,6... | collective-permute-start | bytes 393224 | tf_op jit(solution)/shard_map/ppermute | solution.py:17
Sparse Core Ops, SparseCore 0:
  9.6 38.3 all-gather.3
  91.8 41.0 reduce-scatter.3
  143.5 35.5 all-gather.5
  222.8 41.0 reduce-scatter.5
  274.5 35.5 all-gather.7
  353.8 41.0 reduce-scatter.7
where the time goes:
time: 425 us; the launch traced here: 417 us
  matrix products  177 us (42%)
  waiting for transfers between devices  136 us (32%)
  local copies, waits for them, and re-layouts  51.5 us (12%)
  starting transfers between devices  20.8 us (5%)
  other arithmetic  16.8 us (4%)
  between operations  14.8 us (3%)
    reduce_scatter x3, waiting for transfers between devices, local(): lax.psum_scatter(grad_v, 'user', scatter_dimension=0, tiled=True)  97.4 us
    dot_general x3, matrix products, local_grads(): jnp.einsum('abkir,abkjr->abkij', user_blocks, item_blocks, precision=lax....  48.8 us
    dot_general x3, matrix products, local_grads(): jnp.einsum('abkij,abkir->abkjr', residuals, user_blocks, precision=lax.Pr...  37 us
    dot_general x3, matrix products, local_grads(): jnp.einsum('abkij,abkjr->abkir', residuals, item_blocks, precision=lax.Pr...  35.1 us
    all_gather x3, waiting for transfers between devices, local(): item_group = lax.all_gather(own_items, 'user', axis=0, tiled=True)  33.6 us
    dot_general x3, matrix products, local_grads(): jnp.einsum('abko,abkir->aoir', row_hot, user_terms, precision=lax.Precisi...  32.2 us
    dot_general x3, matrix products, local_grads(): jnp.einsum('abko,abkjr->bojr', col_hot, item_terms, precision=lax.Precisi...  24.3 us
    ppermute x3, starting transfers between devices, passed_along(): return lax.ppermute(block, axis, route)  20.6 us
  transfers between devices with their start and end apart: 9, of which 8 were waited for; matrix products, arithmetic and copies ran while one was open for 26% of the time, Pallas kernels for 0%

commit v1 on v0

v1 whole, which is shorter than its diff:
```python
import functools

import jax
import jax.numpy as jnp
from jax import lax
from jax.experimental import pallas as pl
from jax.experimental.pallas import tpu as pltpu
from jax.sharding import PartitionSpec as P

STEPS = 3
USER_RATE = 0.01
ITEM_RATE = 0.0015
DECAY = 0.05
MESH = pl.DeviceIdType.MESH
F32 = jnp.float32
BF16 = jnp.bfloat16
GROUP = 4
VMEM_LIMIT = 16 << 20
COPY_IN = False


def split(x):
    hi = x.astype(BF16)
    return hi, (x - hi.astype(F32)).astype(BF16)


def chip_array(shape, dtype):
    return pltpu.VMEM(shape, dtype)


def on_chip(x):
    return pltpu.with_memory_space_constraint(x, pltpu.VMEM)


def off_chip(x):
    return pltpu.with_memory_space_constraint(x, pltpu.HBM)


def matmul(a, b, dims=((1,), (0,))):
    return lax.dot_general(a, b, (dims, ((), ())), preferred_element_type=F32)


def grads_kernel(step, idx, cnt, uhl, vhl, ubase, ratings, unew, gv, *refs):
    final, out_sems = (refs[0], refs[-1]) if step == STEPS - 1 else (None, None)
    psc, rsc, tsc = refs[1:4] if step == STEPS - 1 else refs
    rows, cols = cnt.shape[1], cnt.shape[2]
    tiles = rows * cols
    side = psc.shape[1]
    slots = idx.shape[3]
    sub = uhl.shape[0] // rows
    never = 1 << 20

    total = 0
    for t in range(rows):
        for c in range(cols):
            total = total + cnt[step, t, c]
    groups = lax.div(total + (GROUP - 1), GROUP)

    def locate(tile, slot):
        near = jnp.minimum(tile, tiles - 1)
        t, c = lax.div(near, cols), lax.rem(near, cols)
        q = idx[step, t, c, slot]
        last = slot + 1 >= cnt[step, t, c]
        spot = (t * sub + lax.div(q, sub), c * sub + lax.rem(q, sub), near * slots + slot)
        return spot, jnp.where(last, tile + 1, tile), jnp.where(last, 0, slot + 1)

    def group_at(cursor):
        spots, floors = [], []
        tile, slot = cursor
        for _ in range(GROUP):
            floors.append(jnp.where(tile < tiles, 0, never))
            spot, tile, slot = locate(tile, slot)
            spots += spot
        return (*spots, *floors), (tile, slot)

    def predict(group):
        for g in range(GROUP):
            row, item = group[3 * g], group[3 * g + 1]
            parts = matmul(uhl[row], vhl[item], ((1,), (1,)))
            psc[g] = parts[:side, :side] + (parts[:side, side:] + parts[side:, :side])

    def residual(group, over):
        for g in range(GROUP):
            rating = ratings[group[3 * g + 2]]
            floor = jnp.where(over, never, group[3 * GROUP + g])
            res = jnp.where(rating > floor, 0.5 * rating.astype(F32) - psc[g], 0.0)
            for into, x in ((rsc, res), (tsc, res.T)):
                hi, lo = split(x)
                into[g, 0] = hi
                into[g, 1] = lo

    def product(left, g, right):
        hi, lo = left[g, 0], left[g, 1]
        twice = jnp.concatenate(
            [jnp.concatenate([hi, hi], axis=1), jnp.concatenate([lo, lo], axis=1)], axis=0
        )
        both = matmul(twice, right[...])
        return both[:side] + both[side:]

    def update(group):
        for g in range(GROUP):
            row, item = group[3 * g], group[3 * g + 1]
            unew[row] += USER_RATE * product(rsc, g, vhl.at[item])
            gv[item] += product(tsc, g, uhl.at[row])

    def put(row):
        part = pl.ds(row * sub, sub)
        return pltpu.make_async_copy(unew.at[part], final.at[part], out_sems.at[row])

    def start_put(row, carry):
        put(row).start()
        return carry

    gv[...] = jnp.zeros_like(gv)
    if COPY_IN:
        unew[...] = ubase[...]
    one, cursor = group_at((jnp.int32(0), jnp.int32(0)))
    predict(one)
    residual(one, False)
    two, cursor = group_at(cursor)
    predict(two)

    def body(i, carry):
        now, coming, cursor = carry
        fresh, cursor = group_at(cursor)
        update(now)
        residual(coming, i + 1 >= groups)
        predict(fresh)
        if final is not None:
            here, there = (lax.div(group[2], cols * slots) for group in (now, coming))
            lax.fori_loop(here, jnp.where(i + 1 >= groups, rows, there), start_put, 0)
        return coming, fresh, cursor

    lax.fori_loop(0, groups, body, (one, two, cursor))
    if final is not None:
        for row in range(rows):
            put(row).wait()


def local_grads(step, idx, cnt, uhl, vhl, ubase, ratings):
    side = ratings.shape[-1]
    rank = ubase.shape[-1]
    vmem = pl.BlockSpec(memory_space=pltpu.VMEM)
    smem = pl.BlockSpec(memory_space=pltpu.SMEM)
    outs = [chip_array(ubase.shape, F32), chip_array((vhl.shape[0], side, rank), F32)]
    out_specs = [vmem, vmem]
    scratch = [pltpu.VMEM((GROUP, side, side), F32)] + [pltpu.VMEM((GROUP, 2, side, side), BF16)] * 2
    if step == STEPS - 1:
        outs.append(jax.ShapeDtypeStruct(ubase.shape, F32))
        out_specs.append(pl.BlockSpec(memory_space=pl.ANY))
        scratch.append(pltpu.SemaphoreType.DMA((cnt.shape[1],)))
    return pl.pallas_call(
        functools.partial(grads_kernel, step),
        out_shape=tuple(outs),
        in_specs=[smem, smem, vmem, vmem, vmem, vmem],
        out_specs=tuple(out_specs),
        scratch_shapes=scratch,
        input_output_aliases={4: 0},
        compiler_params=pltpu.CompilerParams(vmem_limit_bytes=VMEM_LIMIT),
        name=f"grads{step}",
    )(idx, cnt, on_chip(uhl), on_chip(vhl), on_chip(ubase), on_chip(ratings))


class Links:
    def __init__(self, sends, recvs):
        self.sends, self.recvs = sends, recvs
        self.started = []
        self.count = 0

    def message(self):
        self.count += 1
        return self.count - 1

    def copy(self, number, src, dst, device):
        return pltpu.make_async_remote_copy(
            src_ref=src,
            dst_ref=dst,
            send_sem=self.sends.at[number],
            recv_sem=self.recvs.at[number],
            device_id=device,
            device_id_type=MESH,
        )

    def send(self, number, src, dst, device):
        copy = self.copy(number, src, dst, device)
        copy.start()
        self.started.append(copy)

    def arrived(self, number, dst, device):
        self.copy(number, dst, dst, device).wait_recv()


PARTS = ((0, 48), (48, 48), (96, 32))


def part_halves(part):
    first, size = part
    return (pl.ds(first, size // 2), pl.ds(first + size // 2, size // 2))


def exchange_kernel(step, reduce, gather, *refs):
    refs = list(refs)
    gv = refs.pop(0) if reduce else None
    vin = refs.pop(0)
    uin, rin_hbm = (refs.pop(0), refs.pop(0)) if gather else (None, None)
    vout = refs.pop(0) if reduce else None
    vhl, uhl, ubase, rout = (refs.pop(0) for _ in range(4)) if gather else (None,) * 4
    if reduce:
        xin, xsum, opp, stage, rin, xio, vnew = (refs.pop(0) for _ in range(7))
    if gather:
        vx, vy, vo = (refs.pop(0) for _ in range(3))
    if gather and not reduce:
        uraw = refs.pop(0)
    if gather:
        load_sems, rate_sem = refs.pop(0), refs.pop(0)
    sends, recvs = refs

    loads = []
    if gather:
        if not reduce:
            span = uin.shape[0] // LOADS
            for i in range(LOADS):
                piece = pl.ds(i * span, span)
                loads.append(pltpu.make_async_copy(uin.at[piece], uraw.at[piece], load_sems.at[i]))
            for load in loads:
                load.start()
            uin = uraw
        rates = pltpu.make_async_copy(rin_hbm.at[step], rout, rate_sem)
        rates.start()

    blk, user = lax.axis_index("blk"), lax.axis_index("user")
    blks = lax.axis_size("blk")
    y, xl = lax.div(user, 2), lax.rem(user, 2)
    ys = lax.axis_size("user") // 2
    up, down, across = lax.rem(y + 1, ys), lax.rem(y + ys - 1, ys), lax.rem(y + 2, ys)
    near = (up, down)
    to_y = ((blk, up * 2 + xl), (blk, down * 2 + xl))
    from_y = (to_y[1], to_y[0])
    to_x = (blk, y * 2 + 1 - xl)
    after = (lax.rem(blk + 1, blks), user)
    before = (lax.rem(blk + blks - 1, blks), user)

    def number(row, which):
        return row * 2 + (1 - xl if which == 0 else xl)

    side = vin.shape[0]
    halves = [part_halves(part) for part in PARTS]
    whole = [pl.ds(*part) for part in PARTS]
    links = Links(sends, recvs)
    both = (0, 1)

    done = [0]

    def user_work(amount):
        if not gather:
            return
        blocks = uin.shape[0]
        start = done[0]
        stop = min(blocks, start + amount)
        done[0] = stop
        if start == stop:
            return
        while loads and (LOADS - len(loads)) * (blocks // LOADS) < stop:
            loads.pop(0).wait()

        def one(i, carry):
            x = uin[i]
            hi, lo = split(x)
            uhl[i, :side] = hi
            uhl[i, side:] = lo
            ubase[i] = x * (1.0 - USER_RATE * DECAY)
            return carry

        lax.fori_loop(start, stop, one, 0)

    barrier = pltpu.get_barrier_semaphore()
    greet = [to_y[0], to_y[1], to_x] + ([before] if reduce else [])
    for device in greet:
        pl.semaphore_signal(barrier, inc=1, device_id=device, device_id_type=MESH)
    pl.semaphore_wait(barrier, len(greet))

    ids = {}

    def number_of(*key):
        if key not in ids:
            ids[key] = links.message()
        return ids[key]

    def send(key, src, dst, device):
        links.send(number_of(*key), src, dst, device)

    def arrived(key, dst, device):
        links.arrived(number_of(*key), dst, device)


    def first_sends(p):
        for w in both:
            for d in both:
                send(("A", p, d, w), gv.at[number(across, w), halves[p][d]], opp.at[d, w, halves[p][d]], to_y[d])
        for w in both:
            for d in both:
                rows = halves[p][1 - d]
                send(("B", p, d, w), gv.at[number(near[d], w), rows], rin.at[d, w, rows], to_y[d])

    def second_sends(p):
        for w in both:
            for d in both:
                rows = halves[p][d]
                arrived(("A", p, d, w), opp.at[d, w, rows], from_y[d])
                stage[d, w, rows] = gv[number(near[d], w), rows] + opp[d, w, rows]
                send(("C", p, d, w), stage.at[d, w, rows], rin.at[d, w, rows], to_y[d])

    def received(p, w):
        for d in both:
            arrived(("B", p, d, w), rin.at[d, w, halves[p][1 - d]], from_y[d])
            arrived(("C", p, d, w), rin.at[d, w, halves[p][d]], from_y[d])

    def to_partner(p):
        rows = whole[p]
        received(p, 0)
        xio[0, rows] = gv[number(y, 0), rows] + (rin[0, 0, rows] + rin[1, 0, rows])
        send(("X", p), xio.at[0, rows], xio.at[1, rows], to_x)

    def renew(p, own):
        rows = whole[p]
        received(p, 1)
        grad = own() + (rin[0, 1, rows] + rin[1, 1, rows])
        old = vin[rows]
        vnew[0, rows] = old + ITEM_RATE * (grad - DECAY * old)
        send(("N", p), vnew.at[0, rows], vnew.at[1, rows], after)

    def own_sum(p):
        rows = whole[p]
        arrived(("X", p), xio.at[1, rows], to_x)
        return gv[number(y, 1), rows] + xio[1, rows]


    if gather:
        own = vnew.at[1] if reduce else vin

        def open_part(p):
            rows = whole[p]
            if reduce:
                arrived(("N", p), vnew.at[1, rows], before)
            for d in both:
                send(("GY", p, d, 1), own.at[rows], vy.at[d, 1, rows], to_y[d])
            send(("GX", p, 0), own.at[rows], vx.at[rows], to_x)

        def pass_partner(p):
            rows = whole[p]
            arrived(("GX", p, 0), vx.at[rows], to_x)
            for d in both:
                send(("GY", p, d, 0), vx.at[rows], vy.at[d, 0, rows], to_y[d])

        def pass_on(p, w):
            for d in both:
                arrived(("GY", p, d, w), vy.at[d, w, whole[p]], from_y[d])
                rows = halves[p][d]
                send(("GF", p, d, w), vy.at[d, w, rows], vo.at[w, rows], to_y[d])

        def pass_x(p):
            for d in both:
                send(("GX", p, 1 + d), vy.at[d, 1, whole[p]], vy.at[d, 0, whole[p]], to_x)

        def last(p, w):
            for d in both:
                arrived(("GF", p, d, w), vo.at[w, halves[p][d]], from_y[d])

        def divide(block, ref):
            hi, lo = split(ref[...])
            vhl[block, :side] = hi
            vhl[block, side:] = lo

    if reduce:
        x = 0
        roles = (across, up, down, y)
        for r in range(4):
            send(("S", r), gv.at[number(roles[r], 0), whole[x]], xin.at[r], to_x)
        first_sends(1)

        size = PARTS[x][1]
        cut = (pl.ds(0, size // 2), pl.ds(size // 2, size // 2))

        def with_partner(r):
            arrived(("S", r), xin.at[r], to_x)
            xsum[r] = gv[number(roles[r], 1), whole[x]] + xin[r]

        user_work(4)
        with_partner(0)
        for d in both:
            send(("A", x, d, 1), xsum.at[0, cut[d]], opp.at[d, 1, halves[x][d]], to_y[d])
        for d in both:
            with_partner(1 + d)
            rows = halves[x][1 - d]
            send(("B", x, d, 1), xsum.at[1 + d, cut[1 - d]], rin.at[d, 1, rows], to_y[d])
        second_sends(1)
        first_sends(2)
        for d in both:
            rows = halves[x][d]
            arrived(("A", x, d, 1), opp.at[d, 1, rows], from_y[d])
            stage[d, 1, rows] = xsum[1 + d, cut[d]] + opp[d, 1, rows]
            send(("C", x, d, 1), stage.at[d, 1, rows], rin.at[d, 1, rows], to_y[d])
        with_partner(3)
        user_work(3)
        to_partner(1)
        second_sends(2)
        renew(x, lambda: xsum[3])
        user_work(3)
        renew(1, lambda: own_sum(1))
        to_partner(2)
        if gather:
            open_part(0)
            open_part(1)
        renew(2, lambda: own_sum(2))
    elif gather:
        for p in range(3):
            open_part(p)
        user_work(2)

    if gather:
        user_work(2)
        pass_on(0, 1)
        pass_x(0)
        pass_partner(1)
        if reduce:
            open_part(2)
        pass_on(1, 1)
        user_work(2)
        last(0, 1)
        send(("GX", 0, 3), vo.at[1, whole[0]], vo.at[0, whole[0]], to_x)
        pass_partner(2)
        user_work(2)
        pass_on(1, 0)
        user_work(2)
        pass_on(2, 1)
        user_work(2)
        pass_on(2, 0)
        user_work(32)
        divide(user, own)
        arrived(("GX", 0, 0), vx.at[whole[0]], to_x)
        divide(number(y, 0), vx)
        for d in both:
            divide(number((down, up)[d], 1), vy.at[d, 1])
            arrived(("GX", 0, 1 + d), vy.at[d, 0, whole[0]], to_x)
            divide(number((down, up)[d], 0), vy.at[d, 0])
        if reduce:
            vout[...] = vnew[1]
        arrived(("GX", 0, 3), vo.at[0, whole[0]], to_x)
        for w in (1, 0):
            for p in (1, 2):
                last(p, w)
            divide(number(across, w), vo.at[w])
        rates.wait()
    else:
        for p in range(3):
            arrived(("N", p), vnew.at[1, whole[p]], before)
        vout[...] = vnew[1]
    for copy in links.started:
        copy.wait_send()


MESSAGES = 72
LOADS = 4


def exchange(which, step, gv, own, users_in, ratings):
    reduce, gather = gv is not None, users_in is not None
    side, rank = own.shape
    size = PARTS[0][1]
    vmem = pl.BlockSpec(memory_space=pltpu.VMEM)
    anywhere = pl.BlockSpec(memory_space=pl.ANY)
    args = ([on_chip(gv)] if reduce else []) + [on_chip(own)]
    in_specs = [vmem] * len(args)
    outs, scratch = [], []
    if reduce:
        outs.append(chip_array((side, rank), F32))
        scratch += [
            pltpu.VMEM((4, size, rank), F32),
            pltpu.VMEM((4, size, rank), F32),
            pltpu.VMEM((2, 2, side, rank), F32),
            pltpu.VMEM((2, 2, side, rank), F32),
            pltpu.VMEM((2, 2, side, rank), F32),
            pltpu.VMEM((2, side, rank), F32),
            pltpu.VMEM((2, side, rank), F32),
        ]
    if gather:
        blocks = users_in.shape[0]
        args += [on_chip(users_in) if reduce else off_chip(users_in), off_chip(ratings)]
        in_specs += [vmem if reduce else anywhere, anywhere]
        outs += [
            chip_array((8, 2 * side, rank), BF16),
            chip_array((blocks, 2 * side, rank), BF16),
            chip_array((blocks, side, rank), F32),
            chip_array(ratings.shape[1:], jnp.int32),
        ]
        scratch += [
            pltpu.VMEM((side, rank), F32),
            pltpu.VMEM((2, 2, side, rank), F32),
            pltpu.VMEM((2, side, rank), F32),
        ]
        if not reduce:
            scratch.append(pltpu.VMEM((blocks, side, rank), F32))
        scratch += [pltpu.SemaphoreType.DMA((LOADS,)), pltpu.SemaphoreType.DMA]
    scratch += [pltpu.SemaphoreType.DMA((MESSAGES,))] * 2
    return pl.pallas_call(
        functools.partial(exchange_kernel, step, reduce, gather),
        out_shape=tuple(outs),
        in_specs=in_specs,
        out_specs=(vmem,) * len(outs),
        scratch_shapes=scratch,
        compiler_params=pltpu.CompilerParams(
            collective_id=which, has_side_effects=True, vmem_limit_bytes=VMEM_LIMIT
        ),
        name=f"exchange{which}",
    )(*args)


def local(user_factors, item_factors, block_index, block_count, ratings):
    side = ratings.shape[-1]
    rank = user_factors.shape[1]
    users = user_factors.reshape(-1, side, rank)
    flat = ratings.reshape(STEPS, -1, side, side)
    vhl, uhl, ubase, rates = exchange(0, 0, None, item_factors, users, flat)
    own = item_factors
    for step in range(STEPS):
        users, gv, *final = local_grads(step, block_index, block_count, uhl, vhl, ubase, rates)
        if step < STEPS - 1:
            own, vhl, uhl, ubase, rates = exchange(step + 1, step + 1, gv, own, users, flat)
        else:
            (own,) = exchange(STEPS, 0, gv, own, None, None)
    return (final[0].reshape(user_factors.shape), own)


def solution(mesh):
    in_specs = (
        P(("blk", "user"), None),
        P(("blk", "user"), None),
        P(None, ("blk", "user"), None, None),
        P(None, ("blk", "user"), None),
        P(None, ("blk", "user"), None, None, None, None),
    )
    out_specs = (P(("blk", "user"), None), P(("blk", "user"), None))
    return jax.shard_map(local, mesh=mesh, in_specs=in_specs, out_specs=out_specs, check_vma=False)
```

time: 425 us -> 130 us (0.31)
  the two profiles are of different devices: /device:TPU:1 before, /device:TPU:0 now
where the time goes in v1:
time: 130 us; the launch traced here: 129 us
  Pallas kernels  125 us (96%)
  local copies, waits for them, and re-layouts  3.15 us (2%)
    pallas_call x4, Pallas kernels, exchange(): pl.pallas_call(functools.partial(exchange_kernel, step, reduce, gather),...  106 us
    pallas_call x3, Pallas kernels, local_grads(): pl.pallas_call(functools.partial(grads_kernel, step), out_shape=tuple(out...  19 us
    unnamed x5, local copies, waits for them, and re-layouts  3.15 us

profile of v1, /device:TPU:0, one launch (start us, length us, event | category | flops | bytes accessed | tf_op | source)
XLA Modules:
  0.0 129.1 jit_solution(15968188825811508184)
XLA Ops:
  0.6 0.8 copy.15.cnt
  1.4 0.8 copy.14.idx
  2.2 0.0 copy-start
  2.2 0.9 copy-done
  3.1 17.5 %exchange0.1 = (bf16[8,256,256]{2,1,0:T(8,128)(2,1)S(1)}, bf16[32,256,256]{2,1,0:T(8,128)(2,1)S(1)}, f32[32,128,256]{2,1,0:T(8,128)S(1)}, s32[64,128,128]{2,1,0:T(8,128)S(1)}) custom-call(f32[128,256]{1,0:T(8,128)S(1)} %copy-done, f32[32,128,256]{2,1,0:T(8,128)} %bitcast.6, s32[3,64,128,128]{3,2,1,0:T(8,128)} %bitcast.3), custom_call_target="tpu_custom_call" | custom-call | tf_op jit(solution)/shard_map/exchange0/pallas_call | solution.py:505
  20.6 5.8 %grads0.1 = (f32[32,128,256]{2,1,0:T(8,128)S(1)}, f32[8,128,256]{2,1,0:T(8,128)S(1)}) custom-call(s32[3,8,2,4]{3,2,1,0:T(2,128)S(1)} %copy.14.idx, s32[3,8,2]{2,1,0:T(8,128)S(1)} %copy.15.cnt, bf16[32,256,256]{2,1,0:T(8,128)(2,1)S(1)} %get-tuple-element.22.uhl, bf16[8,256,256]{2,1,0:T(8,128)(2,1)S(1)} %get-tuple-element.23.vhl, ...), custom_call_target="tpu_custom_call", output_to_operand_aliasing={{0}: (4, {})} | custom-call | tf_op jit(solution)/shard_map/grads0/pallas_call | solution.py:152
  26.5 33.9 %exchange1.1 = (f32[128,256]{1,0:T(8,128)S(1)}, bf16[8,256,256]{2,1,0:T(8,128)(2,1)S(1)}, bf16[32,256,256]{2,1,0:T(8,128)(2,1)S(1)}, f32[32,128,256]{2,1,0:T(8,128)S(1)}, s32[64,128,128]{2,1,0:T(8,128)S(1)}) custom-call(f32[8,128,256]{2,1,0:T(8,128)S(1)} %get-tuple-element.26.refs_0_, f32[128,256]{1,0:T(8,128)S(1)} %copy-done, ...), custom_call_target="tpu_custom_call" | custom-call | tf_op jit(solution)/shard_map/exchange1/pallas_call | solution.py:505
  60.4 6.3 %grads1.1 = (f32[32,128,256]{2,1,0:T(8,128)S(1)}, f32[8,128,256]{2,1,0:T(8,128)S(1)}) custom-call(s32[3,8,2,4]{3,2,1,0:T(2,128)S(1)} %copy.14.idx, s32[3,8,2]{2,1,0:T(8,128)S(1)} %copy.15.cnt, bf16[32,256,256]{2,1,0:T(8,128)(2,1)S(1)} %get-tuple-element.28.uhl, bf16[8,256,256]{2,1,0:T(8,128)(2,1)S(1)} %get-tuple-element.29.vhl, ...), custom_call_target="tpu_custom_call", output_to_operand_aliasing={{0}: (4, {})} | custom-call | tf_op jit(solution)/shard_map/grads1/pallas_call | solution.py:152
  66.7 31.3 %exchange2.1 = (f32[128,256]{1,0:T(8,128)S(1)}, bf16[8,256,256]{2,1,0:T(8,128)(2,1)S(1)}, bf16[32,256,256]{2,1,0:T(8,128)(2,1)S(1)}, f32[32,128,256]{2,1,0:T(8,128)S(1)}, s32[64,128,128]{2,1,0:T(8,128)S(1)}) custom-call(f32[8,128,256]{2,1,0:T(8,128)S(1)} %get-tuple-element.32.refs_0_, f32[128,256]{1,0:T(8,128)S(1)} %get-tuple-element.33.refs_1_, ...), custom_call_target="tpu_custom_call" | custom-call | tf_op jit(solution)/shard_map/exchange2/pallas_call | solution.py:505
  98.1 6.9 %grads2.1 = (f32[32,128,256]{2,1,0:T(8,128)S(1)}, f32[8,128,256]{2,1,0:T(8,128)S(1)}, f32[32,128,256]{2,1,0:T(8,128)}) custom-call(s32[3,8,2,4]{3,2,1,0:T(2,128)S(1)} %copy.14.idx, s32[3,8,2]{2,1,0:T(8,128)S(1)} %copy.15.cnt, bf16[32,256,256]{2,1,0:T(8,128)(2,1)S(1)} %get-tuple-element.35.uhl, ...), custom_call_target="tpu_custom_call", output_to_operand_aliasing={{0}: (4, {})} | custom-call | tf_op jit(solution)/shard_map/grads2/pallas_call | solution.py:152
  104.9 23.5 %exchange3.1 = f32[128,256]{1,0:T(8,128)S(1)} custom-call(f32[8,128,256]{2,1,0:T(8,128)S(1)} %get-tuple-element.40.refs_0_, f32[128,256]{1,0:T(8,128)S(1)} %get-tuple-element.41.refs_1_), custom_call_target="tpu_custom_call" | custom-call | tf_op jit(solution)/shard_map/exchange3/pallas_call | solution.py:505
  128.5 0.7 copy.20
Async XLA Ops:
  2.2 0.9 copy-start

commit v2 on v1

--- a/solution.py
+++ b/solution.py
@@ -43,24 +43,24 @@
 def grads_kernel(step, idx, cnt, uhl, vhl, ubase, ratings, unew, gv, *refs):
     final, out_sems = (refs[0], refs[-1]) if step == STEPS - 1 else (None, None)
     psc, rsc, tsc = refs[1:4] if step == STEPS - 1 else refs
-    rows, cols = cnt.shape[1], cnt.shape[2]
+    cols, rows = cnt.shape[1], cnt.shape[2]
     tiles = rows * cols
     side = psc.shape[1]
-    slots = idx.shape[3]
+    slots = idx.shape[2]
     sub = uhl.shape[0] // rows
     never = 1 << 20
 
     total = 0
     for t in range(rows):
         for c in range(cols):
-            total = total + cnt[step, t, c]
+            total = total + cnt[step, c, t]
     groups = lax.div(total + (GROUP - 1), GROUP)
 
     def locate(tile, slot):
         near = jnp.minimum(tile, tiles - 1)
         t, c = lax.div(near, cols), lax.rem(near, cols)
-        q = idx[step, t, c, slot]
-        last = slot + 1 >= cnt[step, t, c]
+        q = idx[step, c, slot, t]
+        last = slot + 1 >= cnt[step, c, t]
         spot = (t * sub + lax.div(q, sub), c * sub + lax.rem(q, sub), near * slots + slot)
         return spot, jnp.where(last, tile + 1, tile), jnp.where(last, 0, slot + 1)
 
@@ -148,7 +148,7 @@
     if step == STEPS - 1:
         outs.append(jax.ShapeDtypeStruct(ubase.shape, F32))
         out_specs.append(pl.BlockSpec(memory_space=pl.ANY))
-        scratch.append(pltpu.SemaphoreType.DMA((cnt.shape[1],)))
+        scratch.append(pltpu.SemaphoreType.DMA((cnt.shape[2],)))
     return pl.pallas_call(
         functools.partial(grads_kernel, step),
         out_shape=tuple(outs),
@@ -190,7 +190,89 @@
         self.copy(number, dst, dst, device).wait_recv()
 
 
-PARTS = ((0, 48), (48, 48), (96, 32))
+PARTS = (("X", 0, 48), ("Y", 48, 48), ("Y", 96, 32))
+GATHER_ORDER = (
+    ("GY", 0, 1),
+    ("GX", 1, 0),
+    ("GY", 2, 1),
+    ("GX", 2, 0),
+    ("GX", 0, 0),
+    ("GY", 1, 1),
+    ("GF", 0, 1),
+    ("GY", 1, 0),
+    ("GX", 0, 1),
+    ("GY", 2, 0),
+    ("GX", 0, 2),
+    ("GF", 2, 1),
+    ("GF", 1, 1),
+    ("GF", 1, 0),
+    ("GF", 2, 0),
+)
+FULL_ORDER = (
+    ("A", 1, 0),
+    ("S", 0, 0),
+    ("A", 2, 1),
+    ("B", 2, 0),
+    ("A", 2, 0),
+    ("B", 1, 0),
+    ("S", 0, 1),
+    ("C", 1, 0),
+    ("A", 1, 1),
+    ("A", 0, 1),
+    ("S", 0, 2),
+    ("B", 1, 1),
+    ("C", 2, 0),
+    ("X", 1),
+    ("C", 1, 1),
+    ("C", 0, 1),
+    ("B", 0, 1),
+    ("X", 2),
+    ("C", 2, 1),
+    ("B", 2, 1),
+    ("N", 1),
+    ("N", 0),
+    ("N", 2),
+    ("GY", 1, 1),
+    ("GX", 1, 0),
+    ("GY", 0, 1),
+    ("GX", 2, 0),
+    ("GY", 2, 1),
+    ("GY", 1, 0),
+    ("GX", 0, 0),
+    ("GX", 0, 1),
+    ("GF", 0, 1),
+    ("GY", 2, 0),
+    ("GF", 2, 1),
+    ("GF", 1, 0),
+    ("GF", 1, 1),
+    ("GX", 0, 2),
+    ("GF", 2, 0),
+)
+REDUCE_ORDER = (
+    ("A", 1, 0),
+    ("S", 0, 0),
+    ("B", 2, 0),
+    ("A", 2, 0),
+    ("S", 0, 1),
+    ("B", 1, 0),
+    ("A", 1, 1),
+    ("C", 1, 0),
+    ("A", 2, 1),
+    ("S", 0, 2),
+    ("A", 0, 1),
+    ("C", 2, 0),
+    ("B", 1, 1),
+    ("C", 1, 1),
+    ("X", 1),
+    ("B", 0, 1),
+    ("C", 0, 1),
+    ("X", 2),
+    ("C", 2, 1),
+    ("B", 2, 1),
+    ("N", 1),
+    ("N", 0),
+    ("N", 2),
+)
 
 
 def part_halves(part):
@@ -203,7 +285,7 @@
     gv = refs.pop(0) if reduce else None
     vin = refs.pop(0)
     uin, rin_hbm = (refs.pop(0), refs.pop(0)) if gather else (None, None)
-    vout = refs.pop(0) if reduce else None
+    vout = refs.pop(0)
     vhl, uhl, ubase, rout = (refs.pop(0) for _ in range(4)) if gather else (None,) * 4
     if reduce:
         xin, xsum, opp, stage, rin, xio, vnew = (refs.pop(0) for _ in range(7))
@@ -212,21 +294,26 @@
     if gather and not reduce:
         uraw = refs.pop(0)
     if gather:
-        load_sems, rate_sem = refs.pop(0), refs.pop(0)
+        load_sems, rate_sem, own_sem = refs.pop(0), refs.pop(0), refs.pop(0)
     sends, recvs = refs
 
     loads = []
     if gather:
-        if not reduce:
-            span = uin.shape[0] // LOADS
-            for i in range(LOADS):
-                piece = pl.ds(i * span, span)
-                loads.append(pltpu.make_async_copy(uin.at[piece], uraw.at[piece], load_sems.at[i]))
-            for load in loads:
-                load.start()
-            uin = uraw
+        uwork = uin if reduce else uraw
         rates = pltpu.make_async_copy(rin_hbm.at[step], rout, rate_sem)
-        rates.start()
+        kept = pltpu.make_async_copy(vin, vout, own_sem)
+
+    def start_loads():
+        if gather:
+            if not reduce:
+                kept.start()
+                span = uin.shape[0] // LOADS
+                for i in range(LOADS):
+                    piece = pl.ds(i * span, span)
+                    loads.append(pltpu.make_async_copy(uin.at[piece], uraw.at[piece], load_sems.at[i]))
+                for load in loads:
+                    load.start()
+            rates.start()
 
     blk, user = lax.axis_index("blk"), lax.axis_index("user")
     blks = lax.axis_size("blk")
@@ -244,8 +331,9 @@
         return row * 2 + (1 - xl if which == 0 else xl)
 
     side = vin.shape[0]
-    halves = [part_halves(part) for part in PARTS]
-    whole = [pl.ds(*part) for part in PARTS]
+    kinds = [kind for kind, first, size in PARTS]
+    halves = [part_halves((first, size)) for kind, first, size in PARTS]
+    whole = [pl.ds(first, size) for kind, first, size in PARTS]
     links = Links(sends, recvs)
     both = (0, 1)
 
@@ -264,7 +352,7 @@
             loads.pop(0).wait()
 
         def one(i, carry):
-            x = uin[i]
+            x = uwork[i]
             hi, lo = split(x)
             uhl[i, :side] = hi
             uhl[i, side:] = lo
@@ -292,191 +380,221 @@
     def arrived(key, dst, device):
         links.arrived(number_of(*key), dst, device)
 
-
-    def first_sends(p):
-        for w in both:
-            for d in both:
-                send(("A", p, d, w), gv.at[number(across, w), halves[p][d]], opp.at[d, w, halves[p][d]], to_y[d])
-        for w in both:
-            for d in both:
-                rows = halves[p][1 - d]
-                send(("B", p, d, w), gv.at[number(near[d], w), rows], rin.at[d, w, rows], to_y[d])
-
-    def second_sends(p):
-        for w in both:
-            for d in both:
-                rows = halves[p][d]
-                arrived(("A", p, d, w), opp.at[d, w, rows], from_y[d])
-                stage[d, w, rows] = gv[number(near[d], w), rows] + opp[d, w, rows]
-                send(("C", p, d, w), stage.at[d, w, rows], rin.at[d, w, rows], to_y[d])
-
-    def received(p, w):
+    def arrived_both(kind, p, w, ref, rows_of):
         for d in both:
-            arrived(("B", p, d, w), rin.at[d, w, halves[p][1 - d]], from_y[d])
-            arrived(("C", p, d, w), rin.at[d, w, halves[p][d]], from_y[d])
-
-    def to_partner(p):
-        rows = whole[p]
-        received(p, 0)
-        xio[0, rows] = gv[number(y, 0), rows] + (rin[0, 0, rows] + rin[1, 0, rows])
-        send(("X", p), xio.at[0, rows], xio.at[1, rows], to_x)
-
-    def renew(p, own):
-        rows = whole[p]
-        received(p, 1)
-        grad = own() + (rin[0, 1, rows] + rin[1, 1, rows])
-        old = vin[rows]
-        vnew[0, rows] = old + ITEM_RATE * (grad - DECAY * old)
-        send(("N", p), vnew.at[0, rows], vnew.at[1, rows], after)
-
-    def own_sum(p):
-        rows = whole[p]
-        arrived(("X", p), xio.at[1, rows], to_x)
-        return gv[number(y, 1), rows] + xio[1, rows]
-
-
+            arrived((kind, p, d, w), ref.at[d, w, rows_of(d)], from_y[d])
+
+    own = None
     if gather:
         own = vnew.at[1] if reduce else vin
-
-        def open_part(p):
-            rows = whole[p]
-            if reduce:
-                arrived(("N", p), vnew.at[1, rows], before)
+    roles = (across, up, down, y)
+
+
+    def send_s(p, r):
+        for role in ((0,), (1, 2), (3,))[r]:
+            at = whole[p]
+            send(("S", p, role), gv.at[number(roles[role], 0), at], xin.at[role, at], to_x)
+
+    def need_s(p, role):
+        at = whole[p]
+        arrived(("S", p, role), xin.at[role, at], to_x)
+        xsum[role, at] = gv[number(roles[role], 1), at] + xin[role, at]
+
+    def ours(p, role, row, w):
+        return xsum.at[role] if kinds[p] == "X" else gv.at[number(row, w)]
+
+    def send_a(p, w):
+        for d in both:
+            at = halves[p][d]
+            send(("A", p, d, w), ours(p, 0, across, w).at[at], opp.at[d, w, at], to_y[d])
+
+    def send_b(p, w):
+        for d in both:
+            at = halves[p][1 - d]
+            send(("B", p, d, w), ours(p, 1 + d, near[d], w).at[at], rin.at[d, w, at], to_y[d])
+
+    def send_c(p, w):
+        for d in both:
+            at = halves[p][d]
+            stage[d, w, at] = ours(p, 1 + d, near[d], w)[at] + opp[d, w, at]
+            send(("C", p, d, w), stage.at[d, w, at], rin.at[d, w, at], to_y[d])
+
+    def send_x(p):
+        at = whole[p]
+        xio[0, at] = gv[number(y, 0), at] + (rin[0, 0, at] + rin[1, 0, at])
+        send(("X", p), xio.at[0, at], xio.at[1, at], to_x)
+
+    def send_n(p):
+        at = whole[p]
+        mine = xsum[3, at] if kinds[p] == "X" else gv[number(y, 1), at] + xio[1, at]
+        grad = mine + (rin[0, 1, at] + rin[1, 1, at])
+        old = vin[at]
+        vnew[0, at] = old + ITEM_RATE * (grad - DECAY * old)
+        send(("N", p), vnew.at[0, at], vnew.at[1, at], after)
+
+    def send_gx(p, k):
+        at = whole[p]
+        if k == 0:
+            send(("GX", p, 0), own.at[at], vx.at[at], to_x)
+        elif k == 1:
             for d in both:
-                send(("GY", p, d, 1), own.at[rows], vy.at[d, 1, rows], to_y[d])
-            send(("GX", p, 0), own.at[rows], vx.at[rows], to_x)
-
-        def pass_partner(p):
-            rows = whole[p]
-            arrived(("GX", p, 0), vx.at[rows], to_x)
+                send(("GX", p, 1 + d), vy.at[d, 1, at], vy.at[d, 0, at], to_x)
+        else:
+            send(("GX", p, 3), vo.at[1, at], vo.at[0, at], to_x)
+
+    def send_gy(p, w):
+        at = whole[p]
+        for d in both:
+            send(("GY", p, d, w), (own if w else vx).at[at], vy.at[d, w, at], to_y[d])
+
+    def send_gf(p, w):
+        for d in both:
+            at = halves[p][d]
+            send(("GF", p, d, w), vy.at[d, w, at], vo.at[w, at], to_y[d])
+
+    waited = set()
+
+    def need(*key):
+        if key in waited:
+            return
+        waited.add(key)
+        kind, p = key[0], key[1]
+        at = whole[p]
+        if kind == "S":
+            for role in ((0,), (1, 2), (3,))[key[2]]:
+                need_s(p, role)
+        elif kind == "A":
+            arrived_both("A", p, key[2], opp, lambda d: halves[p][d])
+        elif kind == "B":
+            arrived_both("B", p, key[2], rin, lambda d: halves[p][1 - d])
+        elif kind == "C":
+            arrived_both("C", p, key[2], rin, lambda d: halves[p][d])
+        elif kind == "X":
+            arrived(("X", p), xio.at[1, at], to_x)
+        elif kind == "N":
+            arrived(("N", p), vnew.at[1, at], before)
+        elif kind == "GX" and key[2] == 0:
+            arrived(("GX", p, 0), vx.at[at], to_x)
+        elif kind == "GX" and key[2] == 1:
             for d in both:
-                send(("GY", p, d, 0), vx.at[rows], vy.at[d, 0, rows], to_y[d])
-
-        def pass_on(p, w):
+                arrived(("GX", p, 1 + d), vy.at[d, 0, at], to_x)
+        elif kind == "GX":
+            arrived(("GX", p, 3), vo.at[0, at], to_x)
+        elif kind == "GY":
+            arrived_both("GY", p, key[2], vy, lambda d: whole[p])
+        elif kind == "GF":
             for d in both:
-                arrived(("GY", p, d, w), vy.at[d, w, whole[p]], from_y[d])
-                rows = halves[p][d]
-                send(("GF", p, d, w), vy.at[d, w, rows], vo.at[w, rows], to_y[d])
-
-        def pass_x(p):
-            for d in both:
-                send(("GX", p, 1 + d), vy.at[d, 1, whole[p]], vy.at[d, 0, whole[p]], to_x)
-
-        def last(p, w):
-            for d in both:
-                arrived(("GF", p, d, w), vo.at[w, halves[p][d]], from_y[d])
-
-        def divide(block, ref):
-            hi, lo = split(ref[...])
-            vhl[block, :side] = hi
-            vhl[block, side:] = lo
-
-    if reduce:
-        x = 0
-        roles = (across, up, down, y)
-        for r in range(4):
-            send(("S", r), gv.at[number(roles[r], 0), whole[x]], xin.at[r], to_x)
-        first_sends(1)
-
-        size = PARTS[x][1]
-        cut = (pl.ds(0, size // 2), pl.ds(size // 2, size // 2))
-
-        def with_partner(r):
-            arrived(("S", r), xin.at[r], to_x)
-            xsum[r] = gv[number(roles[r], 1), whole[x]] + xin[r]
-
-        user_work(4)
-        with_partner(0)
-        for d in both:
-            send(("A", x, d, 1), xsum.at[0, cut[d]], opp.at[d, 1, halves[x][d]], to_y[d])
-        for d in both:
-            with_partner(1 + d)
-            rows = halves[x][1 - d]
-            send(("B", x, d, 1), xsum.at[1 + d, cut[1 - d]], rin.at[d, 1, rows], to_y[d])
-        second_sends(1)
-        first_sends(2)
-        for d in both:
-            rows = halves[x][d]
-            arrived(("A", x, d, 1), opp.at[d, 1, rows], from_y[d])
-            stage[d, 1, rows] = xsum[1 + d, cut[d]] + opp[d, 1, rows]
-            send(("C", x, d, 1), stage.at[d, 1, rows], rin.at[d, 1, rows], to_y[d])
-        with_partner(3)
-        user_work(3)
-        to_partner(1)
-        second_sends(2)
-        renew(x, lambda: xsum[3])
-        user_work(3)
-        renew(1, lambda: own_sum(1))
-        to_partner(2)
-        if gather:
-            open_part(0)
-            open_part(1)
-        renew(2, lambda: own_sum(2))
-    elif gather:
-        for p in range(3):
-            open_part(p)
-        user_work(2)
-
+                arrived(("GF", p, d, key[2]), vo.at[key[2], halves[p][d]], from_y[d])
+
+    def act(kind, p, *rest):
+        x_first = kinds[p] == "X"
+        if kind == "S":
+            send_s(p, *rest)
+        elif kind == "A":
+            if x_first:
+                need("S", p, 0)
+            send_a(p, *rest)
+        elif kind == "B":
+            if x_first:
+                need("S", p, 1)
+            send_b(p, *rest)
+        elif kind == "C":
+            need("A", p, *rest)
+            if x_first:
+                need("S", p, 1)
+            send_c(p, *rest)
+        elif kind == "X":
+            need("B", p, 0)
+            need("C", p, 0)
+            send_x(p)
+        elif kind == "N":
+            need("B", p, 1)
+            need("C", p, 1)
+            need(*(("S", p, 2) if x_first else ("X", p)))
+            send_n(p)
+        elif kind == "GX":
+            if rest[0] == 1:
+                need("GY", p, 1)
+            elif rest[0] == 2:
+                need("GF", p, 1)
+            elif reduce:
+                need("N", p)
+            send_gx(p, *rest)
+        elif kind == "GY":
+            if rest[0] == 0:
+                need("GX", p, 0)
+            elif reduce:
+                need("N", p)
+            send_gy(p, *rest)
+        elif kind == "GF":
+            need("GY", p, *rest)
+            send_gf(p, *rest)
+
+    def divide(block, ref):
+        hi, lo = split(ref[...])
+        vhl[block, :side] = hi
+        vhl[block, side:] = lo
+
+    order = FULL_ORDER if reduce and gather else REDUCE_ORDER if reduce else GATHER_ORDER
+    early = 8 if reduce else 5
+    for turn, action in enumerate(order):
+        act(*action)
+        if turn == early:
+            start_loads()
+        if turn > early:
+            user_work(1)
+    user_work(64)
+
+    parts = range(len(PARTS))
     if gather:
-        user_work(2)
-        pass_on(0, 1)
-        pass_x(0)
-        pass_partner(1)
-        if reduce:
-            open_part(2)
-        pass_on(1, 1)
-        user_work(2)
-        last(0, 1)
-        send(("GX", 0, 3), vo.at[1, whole[0]], vo.at[0, whole[0]], to_x)
-        pass_partner(2)
-        user_work(2)
-        pass_on(1, 0)
-        user_work(2)
-        pass_on(2, 1)
-        user_work(2)
-        pass_on(2, 0)
-        user_work(32)
-        divide(user, own)
-        arrived(("GX", 0, 0), vx.at[whole[0]], to_x)
-        divide(number(y, 0), vx)
-        for d in both:
-            divide(number((down, up)[d], 1), vy.at[d, 1])
-            arrived(("GX", 0, 1 + d), vy.at[d, 0, whole[0]], to_x)
-            divide(number((down, up)[d], 0), vy.at[d, 0])
         if reduce:
             vout[...] = vnew[1]
-        arrived(("GX", 0, 3), vo.at[0, whole[0]], to_x)
+        else:
+            kept.wait()
+        divide(user, own if reduce else vout)
+        for p in parts:
+            need("GX", p, 0)
+        divide(number(y, 0), vx)
         for w in (1, 0):
-            for p in (1, 2):
-                last(p, w)
+            for p in parts:
+                if kinds[p] == "X" and not w:
+                    need("GX", p, 1)
+                else:
+                    need("GY", p, w)
+            for d in both:
+                divide(number((down, up)[d], w), vy.at[d, w])
+        for w in (1, 0):
+            for p in parts:
+                if kinds[p] == "X" and not w:
+                    need("GX", p, 2)
+                else:
+                    need("GF", p, w)
             divide(number(across, w), vo.at[w])
         rates.wait()
     else:
-        for p in range(3):
-            arrived(("N", p), vnew.at[1, whole[p]], before)
+        for p in parts:
+            need("N", p)
         vout[...] = vnew[1]
     for copy in links.started:
         copy.wait_send()
 
 
-MESSAGES = 72
+MESSAGES = 128
 LOADS = 4
 
 
 def exchange(which, step, gv, own, users_in, ratings):
     reduce, gather = gv is not None, users_in is not None
     side, rank = own.shape
-    size = PARTS[0][1]
     vmem = pl.BlockSpec(memory_space=pltpu.VMEM)
     anywhere = pl.BlockSpec(memory_space=pl.ANY)
-    args = ([on_chip(gv)] if reduce else []) + [on_chip(own)]
-    in_specs = [vmem] * len(args)
-    outs, scratch = [], []
+    args = [on_chip(gv), on_chip(own)] if reduce else [off_chip(own)]
+    in_specs = [vmem, vmem] if reduce else [anywhere]
+    outs, scratch = [chip_array((side, rank), F32)], []
     if reduce:
-        outs.append(chip_array((side, rank), F32))
         scratch += [
-            pltpu.VMEM((4, size, rank), F32),
-            pltpu.VMEM((4, size, rank), F32),
+            pltpu.VMEM((4, side, rank), F32),
+            pltpu.VMEM((4, side, rank), F32),
             pltpu.VMEM((2, 2, side, rank), F32),
             pltpu.VMEM((2, 2, side, rank), F32),
             pltpu.VMEM((2, 2, side, rank), F32),
@@ -500,7 +618,7 @@
         ]
         if not reduce:
             scratch.append(pltpu.VMEM((blocks, side, rank), F32))
-        scratch += [pltpu.SemaphoreType.DMA((LOADS,)), pltpu.SemaphoreType.DMA]
+        scratch += [pltpu.SemaphoreType.DMA((LOADS,)), pltpu.SemaphoreType.DMA, pltpu.SemaphoreType.DMA]
     scratch += [pltpu.SemaphoreType.DMA((MESSAGES,))] * 2
     return pl.pallas_call(
         functools.partial(exchange_kernel, step, reduce, gather),
@@ -520,8 +638,9 @@
     rank = user_factors.shape[1]
     users = user_factors.reshape(-1, side, rank)
     flat = ratings.reshape(STEPS, -1, side, side)
-    vhl, uhl, ubase, rates = exchange(0, 0, None, item_factors, users, flat)
-    own = item_factors
+    block_index = block_index.transpose(0, 2, 3, 1)
+    block_count = block_count.transpose(0, 2, 1)
+    own, vhl, uhl, ubase, rates = exchange(0, 0, None, item_factors, users, flat)
     for step in range(STEPS):
         users, gv, *final = local_grads(step, block_index, block_count, uhl, vhl, ubase, rates)
         if step < STEPS - 1:

time: 130 us -> 119 us (0.915)
  Pallas kernels: 125 us -> 117 us
  local copies, waits for them, and re-layouts: 3.15 us -> 0.67 us
    pallas_call x4, Pallas kernels: 106 us -> 100 us  [exchange(): pl.pallas_call(functools.partial(exchange_kernel, step, reduce, gather),...]
    unnamed x5, local copies, waits for them, and re-layouts: 3.15 us -> 0.67 us
    pallas_call x3, Pallas kernels: 19 us -> 17 us  [local_grads(): pl.pallas_call(functools.partial(grads_kernel, step), out_shape=tuple(out...]
where the time goes in v2:
time: 119 us
  Pallas kernels  117 us (98%)
    pallas_call x4, Pallas kernels, exchange(): pl.pallas_call(functools.partial(exchange_kernel, step, reduce, gather),...  100 us
    pallas_call x3, Pallas kernels, local_grads(): pl.pallas_call(functools.partial(grads_kernel, step), out_shape=tuple(out...  17 us

profile of v2, /device:TPU:0, one launch (start us, length us, event | category | flops | bytes accessed | tf_op | source)
XLA Modules:
  0.0 118.6 jit_solution(10009261668598505076)
XLA Ops:
  0.6 0.0 copy-start
  0.6 0.0 copy-start.1
  0.7 18.0 %exchange0.1 = (f32[128,256]{1,0:T(8,128)S(1)}, bf16[8,256,256]{2,1,0:T(8,128)(2,1)S(1)}, bf16[32,256,256]{2,1,0:T(8,128)(2,1)S(1)}, f32[32,128,256]{2,1,0:T(8,128)S(1)}, s32[64,128,128]{2,1,0:T(8,128)S(1)}) custom-call(f32[128,256]{1,0:T(8,128)} %refs_0_.1, f32[32,128,256]{2,1,0:T(8,128)} %bitcast.14, s32[3,64,128,128]{3,2,1,0:T(8,128)} %bitcast.11), custom_call_target="tpu_custom_call" | custom-call | tf_op jit(solution)/shard_map/exchange0/pallas_call | solution.py:623
  18.6 0.0 copy-done
  18.7 0.0 copy-done.1
  18.7 5.4 %grads0.1 = (f32[32,128,256]{2,1,0:T(8,128)S(1)}, f32[8,128,256]{2,1,0:T(8,128)S(1)}) custom-call(s32[3,2,4,8]{3,2,1,0:T(4,128)S(1)} %bitcast.5, s32[3,2,8]{2,1,0:T(2,128)S(1)} %bitcast.8, bf16[32,256,256]{2,1,0:T(8,128)(2,1)S(1)} %get-tuple-element.23.uhl, bf16[8,256,256]{2,1,0:T(8,128)(2,1)S(1)} %get-tuple-element.24.vhl, ...), custom_call_target="tpu_custom_call", output_to_operand_aliasing={{0}: (4, {})} | custom-call | tf_op jit(solution)/shard_map/grads0/pallas_call | solution.py:152
  24.0 31.7 %exchange1.1 = (f32[128,256]{1,0:T(8,128)S(1)}, bf16[8,256,256]{2,1,0:T(8,128)(2,1)S(1)}, bf16[32,256,256]{2,1,0:T(8,128)(2,1)S(1)}, f32[32,128,256]{2,1,0:T(8,128)S(1)}, s32[64,128,128]{2,1,0:T(8,128)S(1)}) custom-call(f32[8,128,256]{2,1,0:T(8,128)S(1)} %get-tuple-element.27.refs_0_, f32[128,256]{1,0:T(8,128)S(1)} %get-tuple-element.28.refs_1_, ...), custom_call_target="tpu_custom_call" | custom-call | tf_op jit(solution)/shard_map/exchange1/pallas_call | solution.py:623
  55.7 5.9 %grads1.1 = (f32[32,128,256]{2,1,0:T(8,128)S(1)}, f32[8,128,256]{2,1,0:T(8,128)S(1)}) custom-call(s32[3,2,4,8]{3,2,1,0:T(4,128)S(1)} %bitcast.6, s32[3,2,8]{2,1,0:T(2,128)S(1)} %bitcast.9, bf16[32,256,256]{2,1,0:T(8,128)(2,1)S(1)} %get-tuple-element.30.uhl, bf16[8,256,256]{2,1,0:T(8,128)(2,1)S(1)} %get-tuple-element.31.vhl, ...), custom_call_target="tpu_custom_call", output_to_operand_aliasing={{0}: (4, {})} | custom-call | tf_op jit(solution)/shard_map/grads1/pallas_call | solution.py:152
  61.6 29.9 %exchange2.1 = (f32[128,256]{1,0:T(8,128)S(1)}, bf16[8,256,256]{2,1,0:T(8,128)(2,1)S(1)}, bf16[32,256,256]{2,1,0:T(8,128)(2,1)S(1)}, f32[32,128,256]{2,1,0:T(8,128)S(1)}, s32[64,128,128]{2,1,0:T(8,128)S(1)}) custom-call(f32[8,128,256]{2,1,0:T(8,128)S(1)} %get-tuple-element.34.refs_0_, f32[128,256]{1,0:T(8,128)S(1)} %get-tuple-element.35.refs_1_, ...), custom_call_target="tpu_custom_call" | custom-call | tf_op jit(solution)/shard_map/exchange2/pallas_call | solution.py:623
  91.5 5.7 %grads2.1 = (f32[32,128,256]{2,1,0:T(8,128)S(1)}, f32[8,128,256]{2,1,0:T(8,128)S(1)}, f32[32,128,256]{2,1,0:T(8,128)}) custom-call(s32[3,2,4,8]{3,2,1,0:T(4,128)S(1)} %bitcast.7, s32[3,2,8]{2,1,0:T(2,128)S(1)} %bitcast.10, bf16[32,256,256]{2,1,0:T(8,128)(2,1)S(1)} %get-tuple-element.37.uhl, ...), custom_call_target="tpu_custom_call", output_to_operand_aliasing={{0}: (4, {})} | custom-call | tf_op jit(solution)/shard_map/grads2/pallas_call | solution.py:152
  97.3 20.6 %exchange3.1 = f32[128,256]{1,0:T(8,128)S(1)} custom-call(f32[8,128,256]{2,1,0:T(8,128)S(1)} %get-tuple-element.42.refs_0_, f32[128,256]{1,0:T(8,128)S(1)} %get-tuple-element.43.refs_1_), custom_call_target="tpu_custom_call" | custom-call | tf_op jit(solution)/shard_map/exchange3/pallas_call | solution.py:623
  117.9 0.7 copy.14
Async XLA Ops:
  0.6 18.0 %copy-start = (s32[3,8,2,4]{1,3,2,0:T(4,128)S(1)}, s32[3,8,2,4]{1,3,2,0:T(4,128)}, u32[]{:S(2)}) copy-start(s32[3,8,2,4]{1,3,2,0:T(4,128)} %param.7) | copy-start | bytes 2308
  0.6 18.0 %copy-start.1 = (s32[3,8,2]{1,2,0:T(2,128)S(1)}, s32[3,8,2]{1,2,0:T(2,128)}, u32[]{:S(2)}) copy-start(s32[3,8,2]{1,2,0:T(2,128)} %param.8) | copy-start | bytes 580

commit v3 on v2

--- a/solution.py
+++ b/solution.py
@@ -191,23 +191,7 @@
 
 
 PARTS = (("X", 0, 48), ("Y", 48, 48), ("Y", 96, 32))
-GATHER_ORDER = (
-    ("GY", 0, 1),
-    ("GX", 1, 0),
-    ("GY", 2, 1),
-    ("GX", 2, 0),
-    ("GX", 0, 0),
-    ("GY", 1, 1),
-    ("GF", 0, 1),
-    ("GY", 1, 0),
-    ("GX", 0, 1),
-    ("GY", 2, 0),
-    ("GX", 0, 2),
-    ("GF", 2, 1),
-    ("GF", 1, 1),
-    ("GF", 1, 0),
-    ("GF", 2, 0),
-)
+EARLY = 8
 FULL_ORDER = (
     ("A", 1, 0),
     ("S", 0, 0),
@@ -301,7 +285,7 @@
     if gather:
         uwork = uin if reduce else uraw
         rates = pltpu.make_async_copy(rin_hbm.at[step], rout, rate_sem)
-        kept = pltpu.make_async_copy(vin, vout, own_sem)
+        kept = None if reduce else pltpu.make_async_copy(vin, vout, own_sem)
 
     def start_loads():
         if gather:
@@ -384,9 +368,7 @@
         for d in both:
             arrived((kind, p, d, w), ref.at[d, w, rows_of(d)], from_y[d])
 
-    own = None
-    if gather:
-        own = vnew.at[1] if reduce else vin
+    own = vnew.at[1] if reduce else vin
     roles = (across, up, down, y)
 
 
@@ -535,46 +517,75 @@
         vhl[block, :side] = hi
         vhl[block, side:] = lo
 
-    order = FULL_ORDER if reduce and gather else REDUCE_ORDER if reduce else GATHER_ORDER
-    early = 8 if reduce else 5
-    for turn, action in enumerate(order):
-        act(*action)
-        if turn == early:
-            start_loads()
-        if turn > early:
-            user_work(1)
-    user_work(64)
-
-    parts = range(len(PARTS))
-    if gather:
-        if reduce:
-            vout[...] = vnew[1]
-        else:
-            kept.wait()
-        divide(user, own if reduce else vout)
-        for p in parts:
-            need("GX", p, 0)
-        divide(number(y, 0), vx)
+    def gather_only():
+        two = (pl.ds(0, side // 2), pl.ds(side // 2, side // 2))
+        for h in both:
+            send(("gx", h), vin.at[two[h]], vx.at[two[h]], to_x)
+            for d in (h, 1 - h):
+                send(("gy", d, 1, h), vin.at[two[h]], vy.at[d, 1, two[h]], to_y[d])
+        start_loads()
+        for h in both:
+            arrived(("gx", h), vx.at[two[h]], to_x)
+            for d in (h, 1 - h):
+                send(("gy", d, 0, h), vx.at[two[h]], vy.at[d, 0, two[h]], to_y[d])
         for w in (1, 0):
-            for p in parts:
-                if kinds[p] == "X" and not w:
-                    need("GX", p, 1)
-                else:
-                    need("GY", p, w)
             for d in both:
+                arrived(("gy", d, w, d), vy.at[d, w, two[d]], from_y[d])
+                send(("gf", d, w), vy.at[d, w, two[d]], vo.at[w, two[d]], to_y[d])
+            if w == 1:
+                divide(number(y, 0), vx)
+                user_work(6)
+        user_work(64)
+        kept.wait()
+        divide(user, vout)
+        for w in (1, 0):
+            for d in both:
+                arrived(("gy", d, w, 1 - d), vy.at[d, w, two[1 - d]], from_y[d])
                 divide(number((down, up)[d], w), vy.at[d, w])
         for w in (1, 0):
-            for p in parts:
-                if kinds[p] == "X" and not w:
-                    need("GX", p, 2)
-                else:
-                    need("GF", p, w)
+            for d in both:
+                arrived(("gf", d, w), vo.at[w, two[d]], from_y[d])
             divide(number(across, w), vo.at[w])
         rates.wait()
-    else:
-        for p in parts:
-            need("N", p)
-        vout[...] = vnew[1]
+
+    def by_parts():
+        order = FULL_ORDER if gather else REDUCE_ORDER
+        for turn, action in enumerate(order):
+            act(*action)
+            if turn == EARLY:
+                start_loads()
+            if turn > EARLY:
+                user_work(1)
+        user_work(64)
+
+        parts = range(len(PARTS))
+        if gather:
+            vout[...] = vnew[1]
+            divide(user, own)
+            for p in parts:
+                need("GX", p, 0)
+            divide(number(y, 0), vx)
+            for w in (1, 0):
+                for p in parts:
+                    if kinds[p] == "X" and not w:
+                        need("GX", p, 1)
+                    else:
+                        need("GY", p, w)
+                for d in both:
+                    divide(number((down, up)[d], w), vy.at[d, w])
+            for w in (1, 0):
+                for p in parts:
+                    if kinds[p] == "X" and not w:
+                        need("GX", p, 2)
+                    else:
+                        need("GF", p, w)
+                divide(number(across, w), vo.at[w])
+            rates.wait()
+        else:
+            for p in parts:
+                need("N", p)
+            vout[...] = vnew[1]
+    by_parts() if reduce else gather_only()
     for copy in links.started:
         copy.wait_send()
 

time: 119 us -> 119 us (level)
  no operation moved by 1% of the time
where the time goes in v3:
time: 119 us; the launch traced here: 118 us
  Pallas kernels  117 us (98%)
    pallas_call x4, Pallas kernels, exchange(): pl.pallas_call(functools.partial(exchange_kernel, step, reduce, gather),...  101 us
    pallas_call x3, Pallas kernels, local_grads(): pl.pallas_call(functools.partial(grads_kernel, step), out_shape=tuple(out...  16 us

profile of v3, /device:TPU:0, one launch (start us, length us, event | category | flops | bytes accessed | tf_op | source)
XLA Modules:
  0.0 118.4 jit_solution(4940495858396745000)
XLA Ops:
  0.6 0.0 copy-start
  0.6 0.0 copy-start.1
  0.7 17.3 %exchange0.1 = (f32[128,256]{1,0:T(8,128)S(1)}, bf16[8,256,256]{2,1,0:T(8,128)(2,1)S(1)}, bf16[32,256,256]{2,1,0:T(8,128)(2,1)S(1)}, f32[32,128,256]{2,1,0:T(8,128)S(1)}, s32[64,128,128]{2,1,0:T(8,128)S(1)}) custom-call(f32[128,256]{1,0:T(8,128)} %refs_0_.1, f32[32,128,256]{2,1,0:T(8,128)} %bitcast.14, s32[3,64,128,128]{3,2,1,0:T(8,128)} %bitcast.11), custom_call_target="tpu_custom_call" | custom-call | tf_op jit(solution)/shard_map/exchange0/pallas_call | solution.py:634
  18.0 0.0 copy-done
  18.0 0.0 copy-done.1
  18.0 5.4 %grads0.1 = (f32[32,128,256]{2,1,0:T(8,128)S(1)}, f32[8,128,256]{2,1,0:T(8,128)S(1)}) custom-call(s32[3,2,4,8]{3,2,1,0:T(4,128)S(1)} %bitcast.5, s32[3,2,8]{2,1,0:T(2,128)S(1)} %bitcast.8, bf16[32,256,256]{2,1,0:T(8,128)(2,1)S(1)} %get-tuple-element.23.uhl, bf16[8,256,256]{2,1,0:T(8,128)(2,1)S(1)} %get-tuple-element.24.vhl, ...), custom_call_target="tpu_custom_call", output_to_operand_aliasing={{0}: (4, {})} | custom-call | tf_op jit(solution)/shard_map/grads0/pallas_call | solution.py:152
  23.3 32.4 %exchange1.1 = (f32[128,256]{1,0:T(8,128)S(1)}, bf16[8,256,256]{2,1,0:T(8,128)(2,1)S(1)}, bf16[32,256,256]{2,1,0:T(8,128)(2,1)S(1)}, f32[32,128,256]{2,1,0:T(8,128)S(1)}, s32[64,128,128]{2,1,0:T(8,128)S(1)}) custom-call(f32[8,128,256]{2,1,0:T(8,128)S(1)} %get-tuple-element.27.refs_0_, f32[128,256]{1,0:T(8,128)S(1)} %get-tuple-element.28.refs_1_, ...), custom_call_target="tpu_custom_call" | custom-call | tf_op jit(solution)/shard_map/exchange1/pallas_call | solution.py:634
  55.8 4.8 %grads1.1 = (f32[32,128,256]{2,1,0:T(8,128)S(1)}, f32[8,128,256]{2,1,0:T(8,128)S(1)}) custom-call(s32[3,2,4,8]{3,2,1,0:T(4,128)S(1)} %bitcast.6, s32[3,2,8]{2,1,0:T(2,128)S(1)} %bitcast.9, bf16[32,256,256]{2,1,0:T(8,128)(2,1)S(1)} %get-tuple-element.30.uhl, bf16[8,256,256]{2,1,0:T(8,128)(2,1)S(1)} %get-tuple-element.31.vhl, ...), custom_call_target="tpu_custom_call", output_to_operand_aliasing={{0}: (4, {})} | custom-call | tf_op jit(solution)/shard_map/grads1/pallas_call | solution.py:152
  60.6 30.8 %exchange2.1 = (f32[128,256]{1,0:T(8,128)S(1)}, bf16[8,256,256]{2,1,0:T(8,128)(2,1)S(1)}, bf16[32,256,256]{2,1,0:T(8,128)(2,1)S(1)}, f32[32,128,256]{2,1,0:T(8,128)S(1)}, s32[64,128,128]{2,1,0:T(8,128)S(1)}) custom-call(f32[8,128,256]{2,1,0:T(8,128)S(1)} %get-tuple-element.34.refs_0_, f32[128,256]{1,0:T(8,128)S(1)} %get-tuple-element.35.refs_1_, ...), custom_call_target="tpu_custom_call" | custom-call | tf_op jit(solution)/shard_map/exchange2/pallas_call | solution.py:634
  91.4 5.9 %grads2.1 = (f32[32,128,256]{2,1,0:T(8,128)S(1)}, f32[8,128,256]{2,1,0:T(8,128)S(1)}, f32[32,128,256]{2,1,0:T(8,128)}) custom-call(s32[3,2,4,8]{3,2,1,0:T(4,128)S(1)} %bitcast.7, s32[3,2,8]{2,1,0:T(2,128)S(1)} %bitcast.10, bf16[32,256,256]{2,1,0:T(8,128)(2,1)S(1)} %get-tuple-element.37.uhl, ...), custom_call_target="tpu_custom_call", output_to_operand_aliasing={{0}: (4, {})} | custom-call | tf_op jit(solution)/shard_map/grads2/pallas_call | solution.py:152
  97.3 20.4 %exchange3.1 = f32[128,256]{1,0:T(8,128)S(1)} custom-call(f32[8,128,256]{2,1,0:T(8,128)S(1)} %get-tuple-element.42.refs_0_, f32[128,256]{1,0:T(8,128)S(1)} %get-tuple-element.43.refs_1_), custom_call_target="tpu_custom_call" | custom-call | tf_op jit(solution)/shard_map/exchange3/pallas_call | solution.py:634
  117.7 0.7 copy.14
Async XLA Ops:
  0.6 17.3 %copy-start = (s32[3,8,2,4]{1,3,2,0:T(4,128)S(1)}, s32[3,8,2,4]{1,3,2,0:T(4,128)}, u32[]{:S(2)}) copy-start(s32[3,8,2,4]{1,3,2,0:T(4,128)} %param.7) | copy-start | bytes 2308
  0.6 17.3 %copy-start.1 = (s32[3,8,2]{1,2,0:T(2,128)S(1)}, s32[3,8,2]{1,2,0:T(2,128)}, u32[]{:S(2)}) copy-start(s32[3,8,2]{1,2,0:T(2,128)} %param.8) | copy-start | bytes 580
